TPU v7x, 128 devices: a whole 4x4x4 slice. The times are simulated.
128 devices in a mesh: req: 16 (over y, x), mlp: 8 (over z, core).
Axes of the slice: x: 4, y: 4, z: 4, core: 2. Of those that a mesh axis runs over, the one named last changes fastest.
Arguments:
- tokens: bfloat16 [16384, 1024], P(('req', 'mlp')), may hold values from -6 to 6
- token_owner: int32 [16384, 1], replicated, may hold values from 0 to 127; in each aligned block of 128 rows (0 to 127, 128 to 255, ...) at most 2 rows name the same one
- token_request: int32 [16384], replicated, may hold values from 0 to 3
- cache_len: int32 [512], P(('req', 'mlp')), may hold values from 1 to 512, 131072 in all
- cache_k: bfloat16 [512, 512, 1024], P(('req', 'mlp')), may hold values from -6 to 6
- cache_v: bfloat16 [512, 512, 1024], P(('req', 'mlp')), may hold values from -12 to 12
- w_qkv: bfloat16 [1024, 3072], replicated, may hold values from -0.1875 to 0.1875
- w_out: bfloat16 [1024, 1024], replicated, may hold values from -0.375 to 0.375
- w_fc1: bfloat16 [1024, 4096], P(None, 'mlp'), may hold values from -0.1875 to 0.1875
- w_fc2: bfloat16 [4096, 1024], P('mlp'), may hold values from -0.09375 to 0.09375
- ln1_gain: float32 [1024], replicated, may hold values from 0.1 to 1.9
- ln1_bias: float32 [1024], replicated, may hold values from -3 to 3
- ln2_gain: float32 [1024], replicated, may hold values from 0.1 to 1.9
- ln2_bias: float32 [1024], replicated, may hold values from -3 to 3
Outputs:
- layer_out: bfloat16 [16384, 1024], P(('req', 'mlp'))
Inputs may be any that keep to these rules, and one draw needn't show every extreme that they name: `token_owner`: in each aligned block of 128 rows (the rows of one device) no owner is named more than 2 times, a bound that some block reaches; every owner is named somewhere. `cache_len`: some request has exactly 512 cached positions.
All inputs are finite; a program needn't handle non-finite values. No bound on the sum of `cache_len` on one device may be relied on, other than what follows from the above.
Results may differ from a plain program's by a relative error of at most 0.01.
Values may be sent and summed in bfloat16 or wider, within the bound.
A program may use at most 128 MiB of HBM per device.

v0:
```python
import jax
import jax.numpy as jnp
from jax import lax
from jax.sharding import PartitionSpec as P

HEADS = 16
epsilon = 1e-05


def layer_norm(values, gain, shift):
    center = values - jnp.mean(values, axis=-1, keepdims=True)
    spread = jnp.mean(center * center, axis=-1, keepdims=True)
    return center * lax.rsqrt(spread + epsilon) * gain + shift


def slot_table(owners_flat, requests_flat, owner_index, devices, tok_dev, capacity):
    owners = owners_flat.reshape(devices, tok_dev)
    requests = requests_flat.reshape(devices, tok_dev)
    mine_mask = (owners == owner_index).astype(jnp.int32)
    ranking = jnp.cumsum(mine_mask, axis=1) - 1
    places = jnp.arange(capacity, dtype=jnp.int32)
    hit_table = mine_mask[:, :, None] * (ranking[:, :, None] == places[None, None, :]).astype(
        jnp.int32
    )
    filled = jnp.sum(hit_table, axis=1)
    positions = jnp.arange(tok_dev, dtype=jnp.int32)
    local_row = jnp.sum(hit_table * positions[None, :, None], axis=1)
    sources = jnp.arange(devices, dtype=jnp.int32)[:, None]
    global_row = jnp.where(filled > 0, sources * tok_dev + local_row, -1).reshape(-1)
    slot_request = jnp.sum(hit_table * requests[:, :, None], axis=1).reshape(-1)
    return (global_row, slot_request, filled.reshape(-1))


def attend(projections, cache_keys, cache_values, lengths, global_row, slot_request, filled):
    slot_count = projections.shape[0]
    width = projections.shape[1] // 3
    head_dim = width // HEADS
    context = cache_keys.shape[1]
    score_scale = head_dim ** (-0.5)
    queries = projections[:, :width].reshape(slot_count, HEADS, head_dim)
    key_new = projections[:, width : 2 * width].reshape(slot_count, HEADS, head_dim)
    value_new = projections[:, 2 * width :].reshape(slot_count, HEADS, head_dim)
    new_mask = (
        (filled[None, :] > 0)
        & (slot_request[None, :] == slot_request[:, None])
        & (global_row[None, :] <= global_row[:, None])
    )
    new_score = (
        jnp.einsum("rhd,shd->hrs", queries, key_new, preferred_element_type=jnp.float32)
        * score_scale
    )
    new_exp = jnp.where(new_mask[None], jnp.exp(new_score), jnp.float32(0.0))
    new_total = jnp.sum(new_exp, axis=-1)
    key_place = jnp.arange(context, dtype=jnp.int32)

    def one_request(items):
        keys_here, values_here, length, request_index = items
        mask = (slot_request[:, None] == request_index) & (key_place[None, :] < length)
        score = (
            jnp.einsum(
                "rhd,khd->hrk",
                queries,
                keys_here.reshape(context, HEADS, head_dim),
                preferred_element_type=jnp.float32,
            )
            * score_scale
        )
        old_exp = jnp.where(mask[None], jnp.exp(score), jnp.float32(0.0))
        old_total = jnp.sum(old_exp, axis=-1)
        total = old_total + new_total
        total = jnp.where(total > 0, total, jnp.float32(1.0))
        weight = (old_exp / total[:, :, None]).astype(jnp.bfloat16)
        part = jnp.einsum(
            "hrk,khd->rhd",
            weight,
            values_here.reshape(context, HEADS, head_dim),
            preferred_element_type=jnp.float32,
        )
        return (part, old_total)

    request_ids = jnp.arange(cache_keys.shape[0], dtype=jnp.int32)
    parts, totals = lax.map(one_request, (cache_keys, cache_values, lengths, request_ids))
    denominator = jnp.sum(totals, axis=0) + new_total
    denominator = jnp.where(denominator > 0, denominator, jnp.float32(1.0))
    new_weight = (new_exp / denominator[:, :, None]).astype(jnp.bfloat16)
    result = jnp.sum(parts, axis=0)
    result = result + jnp.einsum(
        "hrs,shd->rhd", new_weight, value_new, preferred_element_type=jnp.float32
    )
    return result.reshape(slot_count, width).astype(jnp.bfloat16)


def per_device(
    tokens,
    token_owner,
    token_request,
    cache_len,
    cache_k,
    cache_v,
    w_qkv,
    w_out,
    w_fc1,
    w_fc2,
    ln1_gain,
    ln1_bias,
    ln2_gain,
    ln2_bias,
):
    n_req = lax.axis_size("req")
    n_mlp = lax.axis_size("mlp")
    devices = n_req * n_mlp
    owner_index = lax.axis_index("req") * n_mlp + lax.axis_index("mlp")
    tok_dev, width = tokens.shape
    capacity = max(2, 2 * tok_dev // devices)
    slot_count = devices * capacity
    owners_flat = token_owner.reshape(-1)
    my_owners = lax.dynamic_slice_in_dim(owners_flat, owner_index * tok_dev, tok_dev)
    owner_onehot = (my_owners[:, None] == jnp.arange(devices, dtype=jnp.int32)[None, :]).astype(
        jnp.int32
    )
    ranking = jnp.cumsum(owner_onehot, axis=0) - 1
    my_rank = jnp.sum(owner_onehot * ranking, axis=1)
    column = my_owners * capacity + my_rank
    dispatch = (column[:, None] == jnp.arange(slot_count, dtype=jnp.int32)[None, :]).astype(
        jnp.bfloat16
    )
    outgoing = jnp.einsum("tr,td->rd", dispatch, tokens, preferred_element_type=jnp.float32).astype(
        jnp.bfloat16
    )
    arrived = lax.all_to_all(
        outgoing.reshape(devices, capacity, width),
        ("req", "mlp"),
        split_axis=0,
        concat_axis=0,
        tiled=True,
    )
    projections = jnp.dot(
        arrived.reshape(slot_count, width), w_qkv, preferred_element_type=jnp.float32
    ).astype(jnp.bfloat16)
    global_row, slot_request, filled = slot_table(
        owners_flat, token_request, owner_index, devices, tok_dev, capacity
    )
    attended = attend(projections, cache_k, cache_v, cache_len, global_row, slot_request, filled)
    returned = lax.all_to_all(
        attended.reshape(devices, capacity, width),
        ("req", "mlp"),
        split_axis=0,
        concat_axis=0,
        tiled=True,
    )
    attn_rows = jnp.dot(
        dispatch, returned.reshape(slot_count, width), preferred_element_type=jnp.float32
    ).astype(jnp.bfloat16)
    projected_out = jnp.dot(attn_rows, w_out, preferred_element_type=jnp.float32)
    normed = layer_norm(projected_out + tokens.astype(jnp.float32), ln1_gain, ln1_bias).astype(
        jnp.bfloat16
    )
    gathered = lax.all_gather(normed, "mlp", axis=0, tiled=True)
    hidden = jax.nn.gelu(
        jnp.dot(gathered, w_fc1, preferred_element_type=jnp.float32), approximate=False
    ).astype(jnp.bfloat16)
    summed = lax.psum_scatter(
        jnp.dot(hidden, w_fc2, preferred_element_type=jnp.float32).astype(jnp.bfloat16),
        "mlp",
        scatter_dimension=0,
        tiled=True,
    ).astype(jnp.float32)
    return layer_norm(normed.astype(jnp.float32) + summed, ln2_gain, ln2_bias).astype(jnp.bfloat16)


def solution(mesh):
    placed = (
        P(("req", "mlp"), None),
        P(),
        P(),
        P(("req", "mlp")),
        P(("req", "mlp"), None, None),
        P(("req", "mlp"), None, None),
        P(),
        P(),
        P(None, "mlp"),
        P("mlp", None),
        P(),
        P(),
        P(),
        P(),
    )
    return jax.shard_map(
        per_device, mesh=mesh, in_specs=placed, out_specs=P(("req", "mlp"), None), check_vma=False
    )
```

profile of v0, /device:TPU:0, one launch (start us, length us, event | category | flops | bytes accessed | tf_op | source)
XLA Modules:
  0.0 244.5 jit_solution(8810175562565531426)
XLA Ops:
  10.8 11.1 %all-to-all-start = ((bf16[128,2,1024]{2,1,0:T(2,128)(2,1)}), bf16[128,2,1024]{2,1,0:T(2,128)(2,1)S(1)}, u32[]{:S(2)}, u32[]{:S(2)}) async-start(bf16[128,2,1024]{2,1,0:T(2,128)(2,1)} %reshape.262), calls=%async_computation | async-start | bytes 1048576 | tf_op jit(solution)/shard_map/all_to_all | solution.py:130
  23.7 12.0 %all-to-all-done = bf16[128,2,1024]{2,1,0:T(2,128)(2,1)S(1)} async-done(((bf16[128,2,1024]{2,1,0:T(2,128)(2,1)}), bf16[128,2,1024]{2,1,0:T(2,128)(2,1)S(1)}, u32[]{:S(2)}, u32[]{:S(2)}) %all-to-all-start) | async-done | bytes 524320 | tf_op jit(solution)/shard_map/all_to_all | solution.py:130
  35.9 4.6 %convolution_convert_fusion = bf16[256,3072]{1,0:T(8,128)(2,1)S(1)} fusion(bf16[256,1024]{1,0:T(8,128)(2,1)S(1)} %reshape.263, bf16[1024,3072]{1,0:T(8,128)(2,1)} %param.22), kind=kOutput, calls=%fused_computation.18 | convolution fusion | flops 1611399168 | bytes 8388608 | tf_op jit(solution)/shard_map/dot_general | solution.py:137
  42.7 4.1 %fusion.8 = (f32[16,256]{1,0:T(8,128)S(1)}, f32[16,256,256]{1,2,0:T(8,128)}) fusion(pred[256,256]{0,1:T(8,128)(4,1)S(1)} %compare_and_fusion, bf16[256,16,64]{0,2,1:T(8,128)(2,1)} %bitcast.82, bf16[256,16,64]{0,2,1:T(8,128)(2,1)S(1)} %bitcast.85), kind=kOutput, calls=%fused_computation.19 | convolution fusion | flops 137359360 | bytes 5324800 | tf_op jit(solution)/shard_map/rhd,shd->hrs/dot_general | solution.py:49
  46.7 88.6 %while.13 = (s32[]{:T(128)}, f32[4,256,16,64]{1,3,2,0:T(8,128)}, f32[4,16,256]{2,1,0:T(8,128)S(1)}, bf16[4,512,1024]{2,1,0:T(8,128)(2,1)}, s32[4]{0:T(128)S(1)},...) while((s32[]{:T(128)}, f32[4,256,16,64]{1,3,2,0:T(8,128)}, ...), condition=%wide.region_9.10_spmd.clone, body=%wide.region_7.9_spmd.clone.sunk | while | flops 551691008 | bytes 29347476 | solution.py:82
  49.3 2.7 %constant_dynamic-slice_fusion.4 = (bf16[1,512,1024]{2,1,0:T(8,128)(2,1)}, bf16[1,512,1024]{2,1,0:T(8,128)(2,1)S(1)}) fusion(bf16[4,512,1024]{2,1,0:T(8,128)(2,1)} %get-tuple-element.249, s32[]{:T(128)} %get-tuple-element.231, bf16[4,512,1024]{2,1,0:T(8,128)(2,1)} %get-tuple-element.245), kind=kLoop, calls=%fused_computation.12.clone.1 | loop fusion | bytes 4194308 | tf_op jit(solution)/shard_map/while/body/jit(dynamic_index_in_dim)/dynamic_slice | solution.py:82
  54.3 6.5 %fusion.122 = (f32[16,256]{1,0:T(8,128)S(1)}, f32[16,512,256]{2,1,0:T(8,128)}) fusion(pred[256,512]{0,1:T(8,128)(4,1)S(1)} %broadcast_and_fusion.2, bf16[512,16,64]{0,2,1:T(8,128)(2,1)} %bitcast.79, bf16[256,16,64]{0,2,1:T(8,128)(2,1)} %get-tuple-element.250), kind=kOutput, calls=%fused_computation.3.clone.1 | convolution fusion | flops 274722816 | bytes 10108928 | tf_op jit(solution)/shard_map/while/body/eval_jaxpr/rhd,khd->hrk/dot_general | solution.py:60
  62.2 6.7 %fusion.123 = f32[4,256,16,64]{1,3,2,0:T(8,128)} fusion(f32[4,256,16,64]{1,3,2,0:T(8,128)} %get-tuple-element.232, s32[]{:T(128)} %get-tuple-element.231, bf16[512,16,64]{0,2,1:T(8,128)(2,1)} %bitcast.78, f32[16,512,256]{2,1,0:T(8,128)} %get-tuple-element.218, f32[16,256]{1,0:T(8,128)S(1)} %compare_select_fusion.3, ...), kind=kOutput, calls=%fused_computation.6.clone.1 | convolution fusion | flops 276824064 | bytes 10633728 | tf_op jit(solution)/shard_map/while/body/eval_jaxpr/hrk,khd->rhd/dot_general | solution.py:73
  71.6 2.7 %constant_dynamic-slice_fusion.4 = (bf16[1,512,1024]{2,1,0:T(8,128)(2,1)}, bf16[1,512,1024]{2,1,0:T(8,128)(2,1)S(1)}) fusion(bf16[4,512,1024]{2,1,0:T(8,128)(2,1)} %get-tuple-element.249, s32[]{:T(128)} %get-tuple-element.231, bf16[4,512,1024]{2,1,0:T(8,128)(2,1)} %get-tuple-element.245), kind=kLoop, calls=%fused_computation.12.clone.1 | loop fusion | bytes 4194308 | tf_op jit(solution)/shard_map/while/body/jit(dynamic_index_in_dim)/dynamic_slice | solution.py:82
  74.3 2.3 copy.56
  76.6 6.5 %fusion.122 = (f32[16,256]{1,0:T(8,128)S(1)}, f32[16,512,256]{2,1,0:T(8,128)}) fusion(pred[256,512]{0,1:T(8,128)(4,1)S(1)} %broadcast_and_fusion.2, bf16[512,16,64]{0,2,1:T(8,128)(2,1)} %bitcast.79, bf16[256,16,64]{0,2,1:T(8,128)(2,1)} %get-tuple-element.250), kind=kOutput, calls=%fused_computation.3.clone.1 | convolution fusion | flops 274722816 | bytes 10108928 | tf_op jit(solution)/shard_map/while/body/eval_jaxpr/rhd,khd->hrk/dot_general | solution.py:60
  84.4 6.7 %fusion.123 = f32[4,256,16,64]{1,3,2,0:T(8,128)} fusion(f32[4,256,16,64]{1,3,2,0:T(8,128)} %get-tuple-element.232, s32[]{:T(128)} %get-tuple-element.231, bf16[512,16,64]{0,2,1:T(8,128)(2,1)} %bitcast.78, f32[16,512,256]{2,1,0:T(8,128)} %get-tuple-element.218, f32[16,256]{1,0:T(8,128)S(1)} %compare_select_fusion.3, ...), kind=kOutput, calls=%fused_computation.6.clone.1 | convolution fusion | flops 276824064 | bytes 10633728 | tf_op jit(solution)/shard_map/while/body/eval_jaxpr/hrk,khd->rhd/dot_general | solution.py:73
  93.7 2.7 %constant_dynamic-slice_fusion.4 = (bf16[1,512,1024]{2,1,0:T(8,128)(2,1)}, bf16[1,512,1024]{2,1,0:T(8,128)(2,1)S(1)}) fusion(bf16[4,512,1024]{2,1,0:T(8,128)(2,1)} %get-tuple-element.249, s32[]{:T(128)} %get-tuple-element.231, bf16[4,512,1024]{2,1,0:T(8,128)(2,1)} %get-tuple-element.245), kind=kLoop, calls=%fused_computation.12.clone.1 | loop fusion | bytes 4194308 | tf_op jit(solution)/shard_map/while/body/jit(dynamic_index_in_dim)/dynamic_slice | solution.py:82
  98.7 6.5 %fusion.122 = (f32[16,256]{1,0:T(8,128)S(1)}, f32[16,512,256]{2,1,0:T(8,128)}) fusion(pred[256,512]{0,1:T(8,128)(4,1)S(1)} %broadcast_and_fusion.2, bf16[512,16,64]{0,2,1:T(8,128)(2,1)} %bitcast.79, bf16[256,16,64]{0,2,1:T(8,128)(2,1)} %get-tuple-element.250), kind=kOutput, calls=%fused_computation.3.clone.1 | convolution fusion | flops 274722816 | bytes 10108928 | tf_op jit(solution)/shard_map/while/body/eval_jaxpr/rhd,khd->hrk/dot_general | solution.py:60
  106.5 6.7 %fusion.123 = f32[4,256,16,64]{1,3,2,0:T(8,128)} fusion(f32[4,256,16,64]{1,3,2,0:T(8,128)} %get-tuple-element.232, s32[]{:T(128)} %get-tuple-element.231, bf16[512,16,64]{0,2,1:T(8,128)(2,1)} %bitcast.78, f32[16,512,256]{2,1,0:T(8,128)} %get-tuple-element.218, f32[16,256]{1,0:T(8,128)S(1)} %compare_select_fusion.3, ...), kind=kOutput, calls=%fused_computation.6.clone.1 | convolution fusion | flops 276824064 | bytes 10633728 | tf_op jit(solution)/shard_map/while/body/eval_jaxpr/hrk,khd->rhd/dot_general | solution.py:73
  115.8 2.7 %constant_dynamic-slice_fusion.4 = (bf16[1,512,1024]{2,1,0:T(8,128)(2,1)}, bf16[1,512,1024]{2,1,0:T(8,128)(2,1)S(1)}) fusion(bf16[4,512,1024]{2,1,0:T(8,128)(2,1)} %get-tuple-element.249, s32[]{:T(128)} %get-tuple-element.231, bf16[4,512,1024]{2,1,0:T(8,128)(2,1)} %get-tuple-element.245), kind=kLoop, calls=%fused_computation.12.clone.1 | loop fusion | bytes 4194308 | tf_op jit(solution)/shard_map/while/body/jit(dynamic_index_in_dim)/dynamic_slice | solution.py:82
  120.8 6.5 %fusion.122 = (f32[16,256]{1,0:T(8,128)S(1)}, f32[16,512,256]{2,1,0:T(8,128)}) fusion(pred[256,512]{0,1:T(8,128)(4,1)S(1)} %broadcast_and_fusion.2, bf16[512,16,64]{0,2,1:T(8,128)(2,1)} %bitcast.79, bf16[256,16,64]{0,2,1:T(8,128)(2,1)} %get-tuple-element.250), kind=kOutput, calls=%fused_computation.3.clone.1 | convolution fusion | flops 274722816 | bytes 10108928 | tf_op jit(solution)/shard_map/while/body/eval_jaxpr/rhd,khd->hrk/dot_general | solution.py:60
  128.7 6.7 %fusion.123 = f32[4,256,16,64]{1,3,2,0:T(8,128)} fusion(f32[4,256,16,64]{1,3,2,0:T(8,128)} %get-tuple-element.232, s32[]{:T(128)} %get-tuple-element.231, bf16[512,16,64]{0,2,1:T(8,128)(2,1)} %bitcast.78, f32[16,512,256]{2,1,0:T(8,128)} %get-tuple-element.218, f32[16,256]{1,0:T(8,128)S(1)} %compare_select_fusion.3, ...), kind=kOutput, calls=%fused_computation.6.clone.1 | convolution fusion | flops 276824064 | bytes 10633728 | tf_op jit(solution)/shard_map/while/body/eval_jaxpr/hrk,khd->rhd/dot_general | solution.py:73
  135.4 3.7 %reduce_sum.116 = f32[256,16,64]{0,2,1:T(8,128)} reduce(f32[4,256,16,64]{1,3,2,0:T(8,128)} %get-tuple-element.63, f32[]{:T(128)} %constant.28.clone.1), dimensions={0}, to_apply=%region_10.11 | reduce | flops 786432 | bytes 5242884 | tf_op jit(solution)/shard_map/reduce_sum | solution.py:86
  139.3 4.4 %fusion.22 = bf16[256,16,64]{0,2,1:T(8,128)(2,1)} fusion(f32[256,16,64]{0,2,1:T(8,128)} %reduce_sum.116, bf16[256,16,64]{0,2,1:T(8,128)(2,1)S(1)} %bitcast.84, f32[16,256,256]{1,2,0:T(8,128)} %get-tuple-element.148, f32[16,256]{1,0:T(8,128)S(1)} %compare_select_fusion.1, pred[256,256]{0,1:T(8,128)(4,1)S(1)} %compare_and_fusion), kind=kOutput, calls=%fused_computation.43 | convolution fusion | flops 138936320 | bytes 6373376 | tf_op jit(solution)/shard_map/hrs,shd->rhd/dot_general | solution.py:87
  147.1 18.7 %all_to_all.10 = bf16[128,2,1024]{2,1,0:T(2,128)(2,1)S(1)} all-to-all(bf16[128,2,1024]{2,1,0:T(2,128)(2,1)} %convert_element_type.69), channel_id=1, replica_groups=mesh['req'=16,'mlp'=8] {'req','mlp'}, dimensions={0} | all-to-all | bytes 1048576 | tf_op jit(solution)/shard_map/all_to_all | solution.py:144
  167.9 21.2 %all-gather.2.cloned.1.call-done = bf16[1024,1024]{1,0:T(8,128)(2,1)} async-done(((bf16[128,1024]{1,0:T(8,128)(2,1)}), bf16[1024,1024]{1,0:T(8,128)(2,1)}) %all-gather.2.cloned.1.call-update) | async-done | bytes 2097168 | tf_op jit(solution)/shard_map/all_gather | solution.py:158
  189.2 9.7 %convolution_convert_fusion.1 = bf16[1024,1024]{1,0:T(8,128)(2,1)} fusion(bf16[512,1024]{1,0:T(8,128)(2,1)} %param.25, bf16[1024,1024]{1,0:T(8,128)(2,1)} %all-gather.2.cloned.1.call-done, bf16[1024,512]{1,0:T(8,128)(2,1)} %param.24), kind=kOutput, calls=%fused_computation.40 | convolution fusion | flops 2182610944 | bytes 6291456 | tf_op jit(solution)/shard_map/dot_general | solution.py:163
  198.9 34.3 %reduce-scatter.2.cloned.1.call-done = bf16[128,1024]{1,0:T(8,128)(2,1)} async-done(((bf16[1024,1024]{1,0:T(8,128)(2,1)}), bf16[128,1024]{1,0:T(8,128)(2,1)}) %reduce-scatter.2.cloned.1.call-update) | async-done | bytes 262160 | tf_op jit(solution)/shard_map/reduce_scatter | solution.py:162
  (110 shorter events, 40.9 us)
Async XLA Ops:
  6.5 159.5 %copy-start = (bf16[1024,1024]{1,0:T(8,128)(2,1)S(1)}, bf16[1024,1024]{1,0:T(8,128)(2,1)}, u32[]{:S(2)}) copy-start(bf16[1024,1024]{1,0:T(8,128)(2,1)} %param.23) | copy-start | bytes 6291460
  6.5 15.5 %copy-start.3 = (s32[16384,1]{0,1:T(1,128)S(1)}, s32[16384,1]{0,1:T(1,128)}, u32[]{:S(2)}) copy-start(s32[16384,1]{0,1:T(1,128)} %param.17) | copy-start | bytes 196612
  6.5 15.9 %copy-start.6 = (s32[16384]{0:T(1024)S(1)}, s32[16384]{0:T(1024)}, u32[]{:S(2)}) copy-start(s32[16384]{0:T(1024)} %param.18) | copy-start | bytes 196612
  10.8 24.9 %all-to-all-start = ((bf16[128,2,1024]{2,1,0:T(2,128)(2,1)}), bf16[128,2,1024]{2,1,0:T(2,128)(2,1)S(1)}, u32[]{:S(2)}, u32[]{:S(2)}) async-start(bf16[128,2,1024]{2,1,0:T(2,128)(2,1)} %reshape.262), calls=%async_computation | async-start | bytes 1048576 | tf_op jit(solution)/shard_map/all_to_all | solution.py:130
  21.9 167.2 %all-gather.2.cloned.1.call-start = ((), (), s32[]{:S(2)}) async-start(), calls=%async_computation.3 | async-start | bytes 2359296 | tf_op jit(solution)/shard_map/all_gather | solution.py:158
  42.6 4.1 %copy-start.9 = (s32[4]{0:T(128)S(1)}, s32[4]{0:T(128)}, u32[]{:S(2)}) copy-start(s32[4]{0:T(128)} %param.19) | copy-start | bytes 52
  135.4 3.7 %copy-start.1 = (bf16[256,1024]{1,0:T(8,128)(2,1)S(1)}, bf16[256,1024]{1,0:T(8,128)(2,1)}, u32[]{:S(2)}) copy-start(bf16[256,1024]{1,0:T(8,128)(2,1)} %get-tuple-element.144) | copy-start | bytes 1572868
  145.7 20.3 %copy-start.2 = (bf16[128,1024]{1,0:T(8,128)(2,1)S(1)}, bf16[128,1024]{1,0:T(8,128)(2,1)}, u32[]{:S(2)}) copy-start(bf16[128,1024]{1,0:T(8,128)(2,1)} %param.16) | copy-start | bytes 786436
  166.0 0.9 copy-start.4
  166.0 0.9 copy-start.5
  167.9 65.3 %reduce-scatter.2.cloned.1.call-start = ((), (), s32[]{:S(2)}) async-start(), calls=%async_computation.4 | async-start | bytes 2359296 | tf_op jit(solution)/shard_map/reduce_scatter | solution.py:162
  198.8 36.8 %copy-start.7 = (f32[1024]{0:T(1024)S(1)}, f32[1024]{0:T(1024)}, u32[]{:S(2)}) copy-start(f32[1024]{0:T(1024)} %param.29) | copy-start | bytes 12292
  198.8 36.8 %copy-start.8 = (f32[1024]{0:T(1024)S(1)}, f32[1024]{0:T(1024)}, u32[]{:S(2)}) copy-start(f32[1024]{0:T(1024)} %param.28) | copy-start | bytes 12292
Sparse Core Ops, SparseCore 0:
  168.0 21.1 all-gather.1
  199.0 34.1 reduce-scatter.1
where the time goes:
time: 245 us; the launch traced here: 244 us
  matrix products  77.6 us (32%)
  waiting for transfers between devices  67.5 us (28%)
  local copies, waits for them, and re-layouts  39.5 us (16%)
  blocking collectives  18.7 us (8%)
  other arithmetic  16 us (7%)
  between operations  13.7 us (6%)
  starting transfers between devices  11.2 us (5%)
    reduce_scatter x1, waiting for transfers between devices, per_device(): lax.psum_scatter(jnp.dot(hidden, w_fc2, preferred_element_type=jnp.float3...  34.3 us
    dynamic_slice x20, local copies, waits for them, and re-layouts, attend(): lax.map(one_request, (cache_keys, cache_values, lengths, request_ids))  30 us
    dot_general x4, matrix products, one_request(): jnp.einsum('hrk,khd->rhd', weight, values_here.reshape(context, HEADS, he...  26.8 us
    dot_general x4, matrix products, one_request(): jnp.einsum('rhd,khd->hrk', queries, keys_here.reshape(context, HEADS, hea...  26.1 us
    all_gather x1, waiting for transfers between devices, per_device(): gathered = lax.all_gather(normed, 'mlp', axis=0, tiled=True)  21.2 us
    all_to_all x1, blocking collectives, per_device(): lax.all_to_all(attended.reshape(devices, capacity, width), ('req', 'mlp')...  18.7 us
    all_to_all x1, waiting for transfers between devices, per_device(): lax.all_to_all(outgoing.reshape(devices, capacity, width), ('req', 'mlp')...  12 us
    all_to_all x1, starting transfers between devices, per_device(): lax.all_to_all(outgoing.reshape(devices, capacity, width), ('req', 'mlp')...  11.1 us
  transfers between devices with their start and end apart: 3, of which 3 were waited for; matrix products, arithmetic and copies ran while one was open for 1% of the time, Pallas kernels for 0%

commit v1 on v0

--- a/solution.py
+++ b/solution.py
@@ -155,7 +155,22 @@
     normed = layer_norm(projected_out + tokens.astype(jnp.float32), ln1_gain, ln1_bias).astype(
         jnp.bfloat16
     )
-    gathered = lax.all_gather(normed, "mlp", axis=0, tiled=True)
+    size, index, rows = (lax.axis_size("mlp"), lax.axis_index("mlp"), normed.shape[0])
+    forward = [(i, (i + 1) % size) for i in range(size)]
+    left = [(i, (i - 1) % size) for i in range(size)]
+    out = jnp.zeros((*normed.shape[:0], size * rows, *normed.shape[0 + 1 :]), normed.dtype)
+    out = lax.dynamic_update_slice_in_dim(out, normed, index * rows, axis=0)
+    from_left = from_right = normed
+    half = size // 2
+    for turn in range(1, half + 1):
+        from_left = lax.ppermute(from_left, "mlp", forward)
+        out = lax.dynamic_update_slice_in_dim(out, from_left, (index - turn) % size * rows, axis=0)
+        if turn < size - half:
+            from_right = lax.ppermute(from_right, "mlp", left)
+            out = lax.dynamic_update_slice_in_dim(
+                out, from_right, (index + turn) % size * rows, axis=0
+            )
+    gathered = out
     hidden = jax.nn.gelu(
         jnp.dot(gathered, w_fc1, preferred_element_type=jnp.float32), approximate=False
     ).astype(jnp.bfloat16)

time: 245 us -> 246 us (level)
  blocking collectives: 18.7 us -> 0 us
  starting transfers between devices: 11.2 us -> 24.9 us
  local copies, waits for them, and re-layouts: 39.5 us -> 45.1 us
    all_gather x1 -> x0, waiting for transfers between devices: 21.2 us -> none  [per_device(): gathered = lax.all_gather(normed, 'mlp', axis=0, tiled=True)]
    all_to_all x1 -> x0, blocking collectives: 18.7 us -> none  [per_device(): lax.all_to_all(attended.reshape(devices, capacity, width), ('req', 'mlp')...]
    ppermute x0 -> x7, waiting for transfers between devices: none -> 14.8 us  [the longest x4 14.8 us: per_device(): from_left = lax.ppermute(from_left, 'mlp', forward)]
    all_to_all x0 -> x1, waiting for transfers between devices: none -> 13.7 us  [per_device(): lax.all_to_all(attended.reshape(devices, capacity, width), ('req', 'mlp')...]
    ppermute x0 -> x7, starting transfers between devices: none -> 8.88 us  [the longest x3 8.86 us: per_device(): from_right = lax.ppermute(from_right, 'mlp', left)]
    reduce_scatter x1, waiting for transfers between devices: 34.3 us -> 28.5 us  [per_device(): lax.psum_scatter(jnp.dot(hidden, w_fc2, preferred_element_type=jnp.float3...]
    dynamic_update_slice x0 -> x7, local copies, waits for them, and re-layouts: none -> 5.08 us  [the longest x4 2.9 us: per_device(): lax.dynamic_update_slice_in_dim(out, from_left, (index - turn) % size * r...]
    all_to_all x0 -> x1, starting transfers between devices: none -> 4.79 us  [per_device(): lax.all_to_all(attended.reshape(devices, capacity, width), ('req', 'mlp')...]
  transfers between devices with their start and end apart: 3 -> 10, of which waited for: 3 -> 7; matrix products, arithmetic and copies ran while one was open for 1% -> 2% of each run, Pallas kernels for 0% -> 0%
where the time goes in v1:
time: 246 us; the launch traced here: 245 us
  matrix products  77.6 us (32%)
  waiting for transfers between devices  68.9 us (28%)
  local copies, waits for them, and re-layouts  45.1 us (18%)
  starting transfers between devices  24.9 us (10%)
  other arithmetic  14.9 us (6%)
  between operations  13.7 us (6%)
    dynamic_slice x20, local copies, waits for them, and re-layouts, attend(): lax.map(one_request, (cache_keys, cache_values, lengths, request_ids))  30 us
    reduce_scatter x1, waiting for transfers between devices, per_device(): lax.psum_scatter(jnp.dot(hidden, w_fc2, preferred_element_type=jnp.float3...  28.5 us
    dot_general x4, matrix products, one_request(): jnp.einsum('hrk,khd->rhd', weight, values_here.reshape(context, HEADS, he...  26.8 us
    dot_general x4, matrix products, one_request(): jnp.einsum('rhd,khd->hrk', queries, keys_here.reshape(context, HEADS, hea...  26.1 us
    ppermute x4, waiting for transfers between devices, per_device(): from_left = lax.ppermute(from_left, 'mlp', forward)  14.8 us
    all_to_all x1, waiting for transfers between devices, per_device(): lax.all_to_all(attended.reshape(devices, capacity, width), ('req', 'mlp')...  13.7 us
    all_to_all x1, waiting for transfers between devices, per_device(): lax.all_to_all(outgoing.reshape(devices, capacity, width), ('req', 'mlp')...  12 us
    all_to_all x1, starting transfers between devices, per_device(): lax.all_to_all(outgoing.reshape(devices, capacity, width), ('req', 'mlp')...  11.1 us
  transfers between devices with their start and end apart: 10, of which 7 were waited for; matrix products, arithmetic and copies ran while one was open for 2% of the time, Pallas kernels for 0%

profile of v1, /device:TPU:0, one launch (start us, length us, event | category | flops | bytes accessed | tf_op | source)
XLA Modules:
  0.0 245.3 jit_solution(3995212513223911768)
XLA Ops:
  10.8 11.1 %all-to-all-start = ((bf16[128,2,1024]{2,1,0:T(2,128)(2,1)}), bf16[128,2,1024]{2,1,0:T(2,128)(2,1)S(1)}, u32[]{:S(2)}, u32[]{:S(2)}) async-start(bf16[128,2,1024]{2,1,0:T(2,128)(2,1)} %reshape.262), calls=%async_computation | async-start | bytes 1048576 | tf_op jit(solution)/shard_map/all_to_all | solution.py:130
  23.6 12.0 %all-to-all-done = bf16[128,2,1024]{2,1,0:T(2,128)(2,1)S(1)} async-done(((bf16[128,2,1024]{2,1,0:T(2,128)(2,1)}), bf16[128,2,1024]{2,1,0:T(2,128)(2,1)S(1)}, u32[]{:S(2)}, u32[]{:S(2)}) %all-to-all-start) | async-done | bytes 524320 | tf_op jit(solution)/shard_map/all_to_all | solution.py:130
  35.9 4.6 %convolution_convert_fusion = bf16[256,3072]{1,0:T(8,128)(2,1)S(1)} fusion(bf16[256,1024]{1,0:T(8,128)(2,1)S(1)} %reshape.263, bf16[1024,3072]{1,0:T(8,128)(2,1)} %param.22), kind=kOutput, calls=%fused_computation.18 | convolution fusion | flops 1611399168 | bytes 8388608 | tf_op jit(solution)/shard_map/dot_general | solution.py:137
  42.7 4.1 %fusion.8 = (f32[16,256]{1,0:T(8,128)S(1)}, f32[16,256,256]{1,2,0:T(8,128)}) fusion(pred[256,256]{0,1:T(8,128)(4,1)S(1)} %compare_and_fusion, bf16[256,16,64]{0,2,1:T(8,128)(2,1)} %bitcast.82, bf16[256,16,64]{0,2,1:T(8,128)(2,1)S(1)} %bitcast.85), kind=kOutput, calls=%fused_computation.19 | convolution fusion | flops 137359360 | bytes 5324800 | tf_op jit(solution)/shard_map/rhd,shd->hrs/dot_general | solution.py:49
  46.7 88.6 %while.13 = (s32[]{:T(128)}, f32[4,256,16,64]{1,3,2,0:T(8,128)}, f32[4,16,256]{2,1,0:T(8,128)S(1)}, bf16[4,512,1024]{2,1,0:T(8,128)(2,1)}, s32[4]{0:T(128)S(1)},...) while((s32[]{:T(128)}, f32[4,256,16,64]{1,3,2,0:T(8,128)}, ...), condition=%wide.region_9.10_spmd.clone, body=%wide.region_7.9_spmd.clone.sunk | while | flops 551691008 | bytes 29347476 | solution.py:82
  54.3 6.5 %fusion.122 = (f32[16,256]{1,0:T(8,128)S(1)}, f32[16,512,256]{2,1,0:T(8,128)}) fusion(pred[256,512]{0,1:T(8,128)(4,1)S(1)} %broadcast_and_fusion.2, bf16[512,16,64]{0,2,1:T(8,128)(2,1)} %bitcast.79, bf16[256,16,64]{0,2,1:T(8,128)(2,1)} %get-tuple-element.252), kind=kOutput, calls=%fused_computation.3.clone.1 | convolution fusion | flops 274722816 | bytes 10108928 | tf_op jit(solution)/shard_map/while/body/eval_jaxpr/rhd,khd->hrk/dot_general | solution.py:60
  62.2 6.7 %fusion.123 = f32[4,256,16,64]{1,3,2,0:T(8,128)} fusion(f32[4,256,16,64]{1,3,2,0:T(8,128)} %get-tuple-element.234, s32[]{:T(128)} %get-tuple-element.233, bf16[512,16,64]{0,2,1:T(8,128)(2,1)} %bitcast.78, f32[16,512,256]{2,1,0:T(8,128)} %get-tuple-element.220, f32[16,256]{1,0:T(8,128)S(1)} %compare_select_fusion.3, ...), kind=kOutput, calls=%fused_computation.6.clone.1 | convolution fusion | flops 276824064 | bytes 10633728 | tf_op jit(solution)/shard_map/while/body/eval_jaxpr/hrk,khd->rhd/dot_general | solution.py:73
  76.6 6.5 %fusion.122 = (f32[16,256]{1,0:T(8,128)S(1)}, f32[16,512,256]{2,1,0:T(8,128)}) fusion(pred[256,512]{0,1:T(8,128)(4,1)S(1)} %broadcast_and_fusion.2, bf16[512,16,64]{0,2,1:T(8,128)(2,1)} %bitcast.79, bf16[256,16,64]{0,2,1:T(8,128)(2,1)} %get-tuple-element.252), kind=kOutput, calls=%fused_computation.3.clone.1 | convolution fusion | flops 274722816 | bytes 10108928 | tf_op jit(solution)/shard_map/while/body/eval_jaxpr/rhd,khd->hrk/dot_general | solution.py:60
  84.4 6.7 %fusion.123 = f32[4,256,16,64]{1,3,2,0:T(8,128)} fusion(f32[4,256,16,64]{1,3,2,0:T(8,128)} %get-tuple-element.234, s32[]{:T(128)} %get-tuple-element.233, bf16[512,16,64]{0,2,1:T(8,128)(2,1)} %bitcast.78, f32[16,512,256]{2,1,0:T(8,128)} %get-tuple-element.220, f32[16,256]{1,0:T(8,128)S(1)} %compare_select_fusion.3, ...), kind=kOutput, calls=%fused_computation.6.clone.1 | convolution fusion | flops 276824064 | bytes 10633728 | tf_op jit(solution)/shard_map/while/body/eval_jaxpr/hrk,khd->rhd/dot_general | solution.py:73
  98.7 6.5 %fusion.122 = (f32[16,256]{1,0:T(8,128)S(1)}, f32[16,512,256]{2,1,0:T(8,128)}) fusion(pred[256,512]{0,1:T(8,128)(4,1)S(1)} %broadcast_and_fusion.2, bf16[512,16,64]{0,2,1:T(8,128)(2,1)} %bitcast.79, bf16[256,16,64]{0,2,1:T(8,128)(2,1)} %get-tuple-element.252), kind=kOutput, calls=%fused_computation.3.clone.1 | convolution fusion | flops 274722816 | bytes 10108928 | tf_op jit(solution)/shard_map/while/body/eval_jaxpr/rhd,khd->hrk/dot_general | solution.py:60
  106.5 6.7 %fusion.123 = f32[4,256,16,64]{1,3,2,0:T(8,128)} fusion(f32[4,256,16,64]{1,3,2,0:T(8,128)} %get-tuple-element.234, s32[]{:T(128)} %get-tuple-element.233, bf16[512,16,64]{0,2,1:T(8,128)(2,1)} %bitcast.78, f32[16,512,256]{2,1,0:T(8,128)} %get-tuple-element.220, f32[16,256]{1,0:T(8,128)S(1)} %compare_select_fusion.3, ...), kind=kOutput, calls=%fused_computation.6.clone.1 | convolution fusion | flops 276824064 | bytes 10633728 | tf_op jit(solution)/shard_map/while/body/eval_jaxpr/hrk,khd->rhd/dot_general | solution.py:73
  120.8 6.5 %fusion.122 = (f32[16,256]{1,0:T(8,128)S(1)}, f32[16,512,256]{2,1,0:T(8,128)}) fusion(pred[256,512]{0,1:T(8,128)(4,1)S(1)} %broadcast_and_fusion.2, bf16[512,16,64]{0,2,1:T(8,128)(2,1)} %bitcast.79, bf16[256,16,64]{0,2,1:T(8,128)(2,1)} %get-tuple-element.252), kind=kOutput, calls=%fused_computation.3.clone.1 | convolution fusion | flops 274722816 | bytes 10108928 | tf_op jit(solution)/shard_map/while/body/eval_jaxpr/rhd,khd->hrk/dot_general | solution.py:60
  128.7 6.7 %fusion.123 = f32[4,256,16,64]{1,3,2,0:T(8,128)} fusion(f32[4,256,16,64]{1,3,2,0:T(8,128)} %get-tuple-element.234, s32[]{:T(128)} %get-tuple-element.233, bf16[512,16,64]{0,2,1:T(8,128)(2,1)} %bitcast.78, f32[16,512,256]{2,1,0:T(8,128)} %get-tuple-element.220, f32[16,256]{1,0:T(8,128)S(1)} %compare_select_fusion.3, ...), kind=kOutput, calls=%fused_computation.6.clone.1 | convolution fusion | flops 276824064 | bytes 10633728 | tf_op jit(solution)/shard_map/while/body/eval_jaxpr/hrk,khd->rhd/dot_general | solution.py:73
  135.4 3.7 %reduce_sum.116 = f32[256,16,64]{0,2,1:T(8,128)} reduce(f32[4,256,16,64]{1,3,2,0:T(8,128)} %get-tuple-element.63, f32[]{:T(128)} %constant.140.clone.1), dimensions={0}, to_apply=%region_10.11 | reduce | flops 786432 | bytes 5242884 | tf_op jit(solution)/shard_map/reduce_sum | solution.py:86
  139.3 4.4 %fusion.22 = bf16[256,16,64]{0,2,1:T(8,128)(2,1)} fusion(f32[256,16,64]{0,2,1:T(8,128)} %reduce_sum.116, bf16[256,16,64]{0,2,1:T(8,128)(2,1)S(1)} %bitcast.84, f32[16,256,256]{1,2,0:T(8,128)} %get-tuple-element.150, f32[16,256]{1,0:T(8,128)S(1)} %compare_select_fusion.1, pred[256,256]{0,1:T(8,128)(4,1)S(1)} %compare_and_fusion), kind=kOutput, calls=%fused_computation.43 | convolution fusion | flops 138936320 | bytes 6373376 | tf_op jit(solution)/shard_map/hrs,shd->rhd/dot_general | solution.py:87
  147.1 4.8 %all-to-all-start.1 = ((bf16[128,2,1024]{2,1,0:T(2,128)(2,1)}), bf16[128,2,1024]{2,1,0:T(2,128)(2,1)S(1)}, u32[]{:S(2)}, u32[]{:S(2)}) async-start(bf16[128,2,1024]{2,1,0:T(2,128)(2,1)} %convert_element_type.69), calls=%async_computation.1 | async-start | bytes 1048576 | tf_op jit(solution)/shard_map/all_to_all | solution.py:144
  151.9 13.7 %all-to-all-done.1 = bf16[128,2,1024]{2,1,0:T(2,128)(2,1)S(1)} async-done(((bf16[128,2,1024]{2,1,0:T(2,128)(2,1)}), bf16[128,2,1024]{2,1,0:T(2,128)(2,1)S(1)}, u32[]{:S(2)}, u32[]{:S(2)}) %all-to-all-start.1) | async-done | bytes 524320 | tf_op jit(solution)/shard_map/all_to_all | solution.py:144
  170.4 4.1 %collective-permute-done = bf16[128,1024]{1,0:T(8,128)(2,1)S(1)} collective-permute-done((bf16[128,1024]{1,0:T(8,128)(2,1)S(1)}, bf16[128,1024]{1,0:T(8,128)(2,1)S(1)}, u32[]{:S(2)}, u32[]{:S(2)}) %collective-permute-start) | collective-permute-done | bytes 262176 | tf_op jit(solution)/shard_map/ppermute | solution.py:166
  174.4 3.0 %collective-permute-start.3 = (bf16[128,1024]{1,0:T(8,128)(2,1)S(1)}, bf16[128,1024]{1,0:T(8,128)(2,1)S(1)}, u32[]{:S(2)}, u32[]{:S(2)}) collective-permute-start(bf16[128,1024]{1,0:T(8,128)(2,1)S(1)} %collective-permute-done.1), channel_id=1, source_target_pairs={{0,7},{1,0},{2,1},{3,2},{4,3},{5,4},{6,5},{7,6},{8,15},{9,8},{10,9... | collective-permute-start | bytes 786440 | tf_op jit(solution)/shard_map/ppermute | solution.py:169
  177.4 4.0 %collective-permute-done.2 = bf16[128,1024]{1,0:T(8,128)(2,1)S(1)} collective-permute-done((bf16[128,1024]{1,0:T(8,128)(2,1)S(1)}, bf16[128,1024]{1,0:T(8,128)(2,1)S(1)}, u32[]{:S(2)}, u32[]{:S(2)}) %collective-permute-start.2) | collective-permute-done | bytes 262176 | tf_op jit(solution)/shard_map/ppermute | solution.py:166
  182.9 3.0 %collective-permute-start.5 = (bf16[128,1024]{1,0:T(8,128)(2,1)S(1)}, bf16[128,1024]{1,0:T(8,128)(2,1)S(1)}, u32[]{:S(2)}, u32[]{:S(2)}) collective-permute-start(bf16[128,1024]{1,0:T(8,128)(2,1)S(1)} %collective-permute-done.3), channel_id=1, source_target_pairs={{0,7},{1,0},{2,1},{3,2},{4,3},{5,4},{6,5},{7,6},{8,15},{9,8},{10,9... | collective-permute-start | bytes 786440 | tf_op jit(solution)/shard_map/ppermute | solution.py:169
  190.6 4.8 %collective-permute-done.6 = bf16[128,1024]{1,0:T(8,128)(2,1)S(1)} collective-permute-done((bf16[128,1024]{1,0:T(8,128)(2,1)S(1)}, bf16[128,1024]{1,0:T(8,128)(2,1)S(1)}, u32[]{:S(2)}, u32[]{:S(2)}) %collective-permute-start.6) | collective-permute-done | bytes 262176 | tf_op jit(solution)/shard_map/ppermute | solution.py:166
  196.2 9.7 %convolution_convert_fusion.1 = bf16[1024,1024]{1,0:T(8,128)(2,1)} fusion(bf16[512,1024]{1,0:T(8,128)(2,1)} %param.25, bf16[1024,1024]{1,0:T(8,128)(2,1)} %constant_dynamic-update-slice_fusion.7, bf16[1024,512]{1,0:T(8,128)(2,1)} %param.24), kind=kOutput, calls=%fused_computation.40 | convolution fusion | flops 2182610944 | bytes 6291456 | tf_op jit(solution)/shard_map/dot_general | solution.py:178
  205.9 28.5 %reduce-scatter.2.cloned.1.call-done = bf16[128,1024]{1,0:T(8,128)(2,1)} async-done(((bf16[1024,1024]{1,0:T(8,128)(2,1)}), bf16[128,1024]{1,0:T(8,128)(2,1)}) %reduce-scatter.2.cloned.1.call-update) | async-done | bytes 262160 | tf_op jit(solution)/shard_map/reduce_scatter | solution.py:177
  (132 shorter events, 63.3 us)
Async XLA Ops:
  6.5 159.2 %copy-start = (bf16[1024,1024]{1,0:T(8,128)(2,1)S(1)}, bf16[1024,1024]{1,0:T(8,128)(2,1)}, u32[]{:S(2)}) copy-start(bf16[1024,1024]{1,0:T(8,128)(2,1)} %param.23) | copy-start | bytes 6291460
  6.5 15.4 %copy-start.4 = (s32[16384,1]{0,1:T(1,128)S(1)}, s32[16384,1]{0,1:T(1,128)}, u32[]{:S(2)}) copy-start(s32[16384,1]{0,1:T(1,128)} %param.17) | copy-start | bytes 196612
  6.5 15.9 %copy-start.5 = (s32[16384]{0:T(1024)S(1)}, s32[16384]{0:T(1024)}, u32[]{:S(2)}) copy-start(s32[16384]{0:T(1024)} %param.18) | copy-start | bytes 196612
  10.8 24.9 %all-to-all-start = ((bf16[128,2,1024]{2,1,0:T(2,128)(2,1)}), bf16[128,2,1024]{2,1,0:T(2,128)(2,1)S(1)}, u32[]{:S(2)}, u32[]{:S(2)}) async-start(bf16[128,2,1024]{2,1,0:T(2,128)(2,1)} %reshape.262), calls=%async_computation | async-start | bytes 1048576 | tf_op jit(solution)/shard_map/all_to_all | solution.py:130
  42.6 4.1 %copy-start.10 = (s32[4]{0:T(128)S(1)}, s32[4]{0:T(128)}, u32[]{:S(2)}) copy-start(s32[4]{0:T(128)} %param.19) | copy-start | bytes 52
  135.4 3.7 %copy-start.2 = (bf16[256,1024]{1,0:T(8,128)(2,1)S(1)}, bf16[256,1024]{1,0:T(8,128)(2,1)}, u32[]{:S(2)}) copy-start(bf16[256,1024]{1,0:T(8,128)(2,1)} %get-tuple-element.146) | copy-start | bytes 1572868
  145.7 20.1 %copy-start.3 = (bf16[128,1024]{1,0:T(8,128)(2,1)S(1)}, bf16[128,1024]{1,0:T(8,128)(2,1)}, u32[]{:S(2)}) copy-start(bf16[128,1024]{1,0:T(8,128)(2,1)} %param.16) | copy-start | bytes 786436
  147.1 18.5 %all-to-all-start.1 = ((bf16[128,2,1024]{2,1,0:T(2,128)(2,1)}), bf16[128,2,1024]{2,1,0:T(2,128)(2,1)S(1)}, u32[]{:S(2)}, u32[]{:S(2)}) async-start(bf16[128,2,1024]{2,1,0:T(2,128)(2,1)} %convert_element_type.69), calls=%async_computation.1 | async-start | bytes 1048576 | tf_op jit(solution)/shard_map/all_to_all | solution.py:144
  151.9 82.5 %reduce-scatter.2.cloned.1.call-start = ((), (), s32[]{:S(2)}) async-start(), calls=%async_computation.3 | async-start | bytes 2359296 | tf_op jit(solution)/shard_map/reduce_scatter | solution.py:177
  166.5 0.7 copy-start.6
  166.5 0.7 copy-start.7
  167.4 7.0 %copy-start.1 = (bf16[1024,1024]{1,0:T(8,128)(2,1)}, bf16[1024,1024]{1,0:T(8,128)(2,1)S(1)}, u32[]{:S(2)}) copy-start(bf16[1024,1024]{1,0:T(8,128)(2,1)S(1)} %get-tuple-element.140) | copy-start | bytes 6291460
  167.4 7.0 %collective-permute-start = (bf16[128,1024]{1,0:T(8,128)(2,1)S(1)}, bf16[128,1024]{1,0:T(8,128)(2,1)S(1)}, u32[]{:S(2)}, u32[]{:S(2)}) collective-permute-start(bf16[128,1024]{1,0:T(8,128)(2,1)S(1)} %get-tuple-element.141), channel_id=1, source_target_pairs={{0,1},{1,2},{2,3},{3,4},{4,5},{5,6},{6,7},{7,0},{8,9},{9,10},{10,1... | collective-permute-start | bytes 786440 | tf_op jit(solution)/shard_map/ppermute | solution.py:166
  167.4 7.0 %collective-permute-start.1 = (bf16[128,1024]{1,0:T(8,128)(2,1)S(1)}, bf16[128,1024]{1,0:T(8,128)(2,1)S(1)}, u32[]{:S(2)}, u32[]{:S(2)}) collective-permute-start(bf16[128,1024]{1,0:T(8,128)(2,1)S(1)} %get-tuple-element.141), channel_id=1, source_target_pairs={{0,7},{1,0},{2,1},{3,2},{4,3},{5,4},{6,5},{7,6},{8,15},{9,8},{10,9... | collective-permute-start | bytes 786440 | tf_op jit(solution)/shard_map/ppermute | solution.py:169
  174.4 7.0 %collective-permute-start.2 = (bf16[128,1024]{1,0:T(8,128)(2,1)S(1)}, bf16[128,1024]{1,0:T(8,128)(2,1)S(1)}, u32[]{:S(2)}, u32[]{:S(2)}) collective-permute-start(bf16[128,1024]{1,0:T(8,128)(2,1)S(1)} %collective-permute-done), channel_id=1, source_target_pairs={{0,1},{1,2},{2,3},{3,4},{4,5},{5,6},{6,7},{7,0},{8,9},{9,10},{10,1... | collective-permute-start | bytes 786440 | tf_op jit(solution)/shard_map/ppermute | solution.py:166
  174.4 8.4 %collective-permute-start.3 = (bf16[128,1024]{1,0:T(8,128)(2,1)S(1)}, bf16[128,1024]{1,0:T(8,128)(2,1)S(1)}, u32[]{:S(2)}, u32[]{:S(2)}) collective-permute-start(bf16[128,1024]{1,0:T(8,128)(2,1)S(1)} %collective-permute-done.1), channel_id=1, source_target_pairs={{0,7},{1,0},{2,1},{3,2},{4,3},{5,4},{6,5},{7,6},{8,15},{9,8},{10,9... | collective-permute-start | bytes 786440 | tf_op jit(solution)/shard_map/ppermute | solution.py:169
  181.4 7.0 %collective-permute-start.4 = (bf16[128,1024]{1,0:T(8,128)(2,1)S(1)}, bf16[128,1024]{1,0:T(8,128)(2,1)S(1)}, u32[]{:S(2)}, u32[]{:S(2)}) collective-permute-start(bf16[128,1024]{1,0:T(8,128)(2,1)S(1)} %collective-permute-done.2), channel_id=1, source_target_pairs={{0,1},{1,2},{2,3},{3,4},{4,5},{5,6},{6,7},{7,0},{8,9},{9,10},{10,1... | collective-permute-start | bytes 786440 | tf_op jit(solution)/shard_map/ppermute | solution.py:166
  182.9 7.0 %collective-permute-start.5 = (bf16[128,1024]{1,0:T(8,128)(2,1)S(1)}, bf16[128,1024]{1,0:T(8,128)(2,1)S(1)}, u32[]{:S(2)}, u32[]{:S(2)}) collective-permute-start(bf16[128,1024]{1,0:T(8,128)(2,1)S(1)} %collective-permute-done.3), channel_id=1, source_target_pairs={{0,7},{1,0},{2,1},{3,2},{4,3},{5,4},{6,5},{7,6},{8,15},{9,8},{10,9... | collective-permute-start | bytes 786440 | tf_op jit(solution)/shard_map/ppermute | solution.py:169
  188.4 7.0 %collective-permute-start.6 = (bf16[128,1024]{1,0:T(8,128)(2,1)S(1)}, bf16[128,1024]{1,0:T(8,128)(2,1)S(1)}, u32[]{:S(2)}, u32[]{:S(2)}) collective-permute-start(bf16[128,1024]{1,0:T(8,128)(2,1)S(1)} %collective-permute-done.4), channel_id=1, source_target_pairs={{0,1},{1,2},{2,3},{3,4},{4,5},{5,6},{6,7},{7,0},{8,9},{9,10},{10,1... | collective-permute-start | bytes 786440 | tf_op jit(solution)/shard_map/ppermute | solution.py:166
  205.8 30.8 %copy-start.8 = (f32[1024]{0:T(1024)S(1)}, f32[1024]{0:T(1024)}, u32[]{:S(2)}) copy-start(f32[1024]{0:T(1024)} %param.29) | copy-start | bytes 12292
  205.8 30.8 %copy-start.9 = (f32[1024]{0:T(1024)S(1)}, f32[1024]{0:T(1024)}, u32[]{:S(2)}) copy-start(f32[1024]{0:T(1024)} %param.28) | copy-start | bytes 12292
Sparse Core Ops, SparseCore 0:
  206.0 28.2 reduce-scatter.1
